TPU v7x, 256 devices: a whole 4x4x8 slice. The times are simulated.
256 devices in a mesh: user: 16 (over x, y_hi, core), item: 16 (over z, y_lo).
Axes of the slice: x: 4, y: 4 (y_hi: 2, y_lo: 2; y = y_hi * 2 + y_lo), z: 8, core: 2. Of those that a mesh axis runs over, the one named last changes fastest.
Arguments:
- item_factors: float32 [16, 4096, 128], P('item', 'user'), may hold values from -2 to 2
- weights: float32 [128, 256, 128, 128], P('user', 'item'), may hold values from 0 to 100
- tile_ids: int32 [128, 16, 16], P('user', 'item'), may hold values from 0 to 31, as said below
- start_factors: float32 [16384, 128], P('user'), may hold values from -4 to 4
Outputs:
- user_factors: float32 [16384, 128], P('user')
Inputs may be any that keep to these rules, and one draw needn't show every extreme that they name: `tile_ids`: entries of one user block and item block are distinct.
All inputs are finite; a program needn't handle non-finite values.
Results may differ from a plain program's by a relative error of at most 0.0003.
Values sent between devices are 32-bit elements; how exact they have to be, the bound alone decides.
A program may use at most 64 MiB of HBM per device.

v0:
```python
import jax
import jax.numpy as jnp
from jax import lax
from jax.sharding import PartitionSpec as P

ITERS = 3


HIGH = lax.Precision.HIGHEST


def partial_image(chosen, wtiles, vectors):
    blocks, count, tile, rank = chosen.shape
    shaped = vectors.reshape(blocks, tile, rank)
    scores = jnp.einsum("bkjr,bur->bkuj", chosen, shaped, precision=HIGH)
    back = jnp.einsum("bkuj,bkjr->bur", scores * wtiles, chosen, precision=HIGH)
    return back.reshape(blocks * tile, rank)


def local_terms(vectors, gram):
    return (
        jnp.dot(vectors, gram, preferred_element_type=jnp.float32, precision=HIGH) + 1.0 * vectors
    )


def update(state, image):
    solved, resid, direction, norm_now = state
    alpha = norm_now / (jnp.sum(direction * image, axis=1, keepdims=True) + 1e-06)
    solved = solved + alpha * direction
    resid = resid - alpha * image
    norm_next = jnp.sum(resid * resid, axis=1, keepdims=True)
    direction = resid + norm_next / (norm_now + 1e-06) * direction
    return (solved, resid, direction, norm_next)


def local(item_factors, weights, tile_ids, start_factors):
    slab = item_factors[0]
    rank = slab.shape[1]
    tile = weights.shape[2]
    gram = lax.psum(
        jnp.dot(slab.T, slab, preferred_element_type=jnp.float32, precision=HIGH), ("user", "item")
    )
    block = lax.all_gather(slab, "user", axis=0, tiled=True)
    vtiles = block.reshape(-1, tile, rank)
    chosen = jnp.take(vtiles, tile_ids[:, 0, :], axis=0)
    blocks = chosen.shape[0]
    prefs = jnp.where(weights > 0, 1.0 + weights, 0.0)
    rhs_part = jnp.einsum("bkuj,bkjr->bur", prefs, chosen, precision=HIGH).reshape(
        blocks * tile, rank
    )
    start_part = partial_image(chosen, weights, start_factors)
    rhs, image = lax.psum((rhs_part, start_part), "item")
    resid = rhs - image - local_terms(start_factors, gram)
    norm_now = jnp.sum(resid * resid, axis=1, keepdims=True)
    state = (start_factors, resid, resid, norm_now)
    for step in range(ITERS):
        direction = state[2]
        image = lax.psum(partial_image(chosen, weights, direction), "item")
        state = update(state, image + local_terms(direction, gram))
    return state[0]


def solution(mesh):
    in_specs = (
        P("item", "user", None),
        P("user", "item", None, None),
        P("user", "item", None),
        P("user", None),
    )
    out_specs = P("user", None)
    return jax.shard_map(local, mesh=mesh, in_specs=in_specs, out_specs=out_specs, check_vma=False)
```

profile of v0, /device:TPU:8, one launch (start us, length us, event | category | flops | bytes accessed | tf_op | source)
XLA Modules:
  0.0 901.9 jit_solution(9021807846128946891)
XLA Ops:
  7.4 0.0 all-gather.3.cloned.1.call-start
  7.4 0.7 all-gather.3.cloned.1.call-update
  8.1 0.0 all-reduce.7.cloned.1.call-start
  8.1 2.0 fusion.48
  10.1 0.0 all-reduce.7.cloned.1.call-update
  10.2 0.0 all-reduce.15.cloned.1.call-start
  10.2 0.7 compare_and_fusion
  10.9 0.7 compare_select_fusion
  11.6 0.1 reshape.116
  11.7 54.6 %all-gather.3.cloned.1.call-done = f32[1,4096,128]{2,1,0:T(8,128)} async-done(((f32[1,256,128]{2,1,0:T(8,128)}), f32[1,4096,128]{2,1,0:T(8,128)}) %all-gather.3.cloned.1.call-update) | async-done | bytes 2097168 | tf_op jit(solution)/shard_map/all_gather | solution.py:43
  66.2 0.0 copy-start.1
  66.2 6.0 gather_fusion
  72.2 0.0 copy-done.1
  72.2 0.0 copy-start
  72.2 11.9 %fusion.18 = f32[8,16,128,128]{2,3,1,0:T(8,128)S(1)} fusion(f32[8,128,128,1]{2,1,3,0:T(8,128)S(1)} %bitcast.77, f32[8,16,128,128]{3,2,1,0:T(8,128)} %bitcast.67, pred[8,16]{1,0:T(8,128)(4,1)S(1)} %compare_and_fusion), kind=kOutput, calls=%fused_computation.23 | convolution fusion | flops 3223322624 | bytes 17301632 | tf_op jit(solution)/shard_map/bkjr,bur->bkuj/dot_general | solution.py:15
  84.1 0.0 copy-done
  84.1 11.5 %fusion.3 = f32[8,128,128,1]{2,1,3,0:T(8,128)S(1)} fusion(f32[8,16,128,128]{3,2,1,0:T(8,128)} %param.5, f32[8,16,128,128]{2,3,1,0:T(8,128)S(1)} %fusion.18, f32[8,16,128,128]{3,2,1,0:T(8,128)S(1)} %bitcast.74, pred[8,16]{1,0:T(8,128)(4,1)S(1)} %compare_and_fusion), kind=kOutput, calls=%fused_computation.8 | convolution fusion | flops 3225419776 | bytes 25690240 | tf_op jit(solution)/shard_map/bkuj,bkjr->bur/dot_general | solution.py:16
  95.6 11.9 %fusion.4 = f32[8,128,128,1]{2,1,3,0:T(8,128)S(1)} fusion(f32[8,16,128,128]{3,2,1,0:T(8,128)} %param.5, f32[8,16,128,128]{3,2,1,0:T(8,128)S(1)} %bitcast.75, pred[8,16]{1,0:T(8,128)(4,1)S(1)} %compare_and_fusion), kind=kOutput, calls=%fused_computation.9 | convolution fusion | flops 3229614080 | bytes 17301632 | tf_op jit(solution)/shard_map/bkuj,bkjr->bur/dot_general | solution.py:48
  107.5 1.0 copy.5
  108.5 1.0 copy.6
  109.5 0.0 all-reduce.15.cloned.1.call-update
  109.6 0.0 all-reduce.9.cloned.1.call-start
  109.6 0.2 copy.10
  109.8 148.4 %all-reduce.7.cloned.1.call-done = f32[128,128]{1,0:T(8,128)} async-done(((f32[128,128]{1,0:T(8,128)}), f32[128,128]{1,0:T(8,128)}) %all-reduce.7.cloned.1.call-update) | async-done | bytes 65552 | tf_op jit(solution)/shard_map/psum | solution.py:40
  258.2 139.9 %all-reduce.15.cloned.1.call-done = (f32[1024,128]{0,1:T(8,128)}, f32[1024,128]{0,1:T(8,128)}) async-done(((f32[1024,128]{0,1:T(8,128)}, f32[1024,128]{0,1:T(8,128)}), (f32[1024,128]{0,1:T(8,128)}, f32[1024,128]{0,1:T(8,128)})) %all-reduce.15.cloned.1.call-update) | async-done | bytes 1048592 | tf_op jit(solution)/shard_map/psum | solution.py:52
  398.1 1.9 fusion.42
  400.1 0.2 copy.26
  400.2 10.4 %fusion.15 = f32[8,128,16,128]{3,1,2,0:T(8,128)S(1)} fusion(f32[8,128,128,1]{2,1,3,0:T(8,128)S(1)} %bitcast.83, f32[8,16,128,128]{3,2,1,0:T(8,128)} %bitcast.68, pred[8,16]{1,0:T(8,128)(4,1)S(1)} %compare_and_fusion), kind=kOutput, calls=%fused_computation.20 | convolution fusion | flops 3223322624 | bytes 17301632 | tf_op jit(solution)/shard_map/bkjr,bur->bkuj/dot_general | solution.py:15
  410.7 0.0 copy-start.2
  410.7 12.8 %fusion.2 = f32[8,128,128,1]{2,1,3,0:T(8,128)S(1)} fusion(f32[8,16,128,128]{3,2,1,0:T(8,128)} %param.5, f32[8,128,16,128]{3,1,2,0:T(8,128)S(1)} %fusion.15, f32[8,16,128,128]{3,2,1,0:T(8,128)} %bitcast.69, pred[8,16]{1,0:T(8,128)(4,1)S(1)} %compare_and_fusion), kind=kOutput, calls=%fused_computation.6 | convolution fusion | flops 3225419776 | bytes 25690240 | tf_op jit(solution)/shard_map/bkuj,bkjr->bur/dot_general | solution.py:16
  423.5 1.0 copy.27
  424.5 0.0 all-reduce.9.cloned.1.call-update
  424.5 0.0 all-reduce.11.cloned.1.call-start
  424.5 137.9 %all-reduce.9.cloned.1.call-done = f32[1024,128]{0,1:T(8,128)} async-done(((f32[1024,128]{0,1:T(8,128)}), f32[1024,128]{0,1:T(8,128)}) %all-reduce.9.cloned.1.call-update) | async-done | bytes 524304 | tf_op jit(solution)/shard_map/psum | solution.py:58
  562.4 0.0 copy-done.2
  562.4 1.7 multiply_reduce_fusion.3
  564.2 0.1 multiply_reduce_fusion.2
  564.3 0.1 multiply_add_fusion.2
  564.4 0.2 copy.28
  564.6 10.6 %fusion.12 = f32[8,128,16,128]{3,1,2,0:T(8,128)S(1)} fusion(f32[8,128,128,1]{2,1,3,0:T(8,128)S(1)} %bitcast.84, f32[8,16,128,128]{3,2,1,0:T(8,128)} %bitcast.70, pred[8,16]{1,0:T(8,128)(4,1)S(1)} %compare_and_fusion), kind=kOutput, calls=%fused_computation.17 | convolution fusion | flops 3223322624 | bytes 17301632 | tf_op jit(solution)/shard_map/bkjr,bur->bkuj/dot_general | solution.py:15
  575.2 12.7 %fusion.1 = f32[8,128,128,1]{2,1,3,0:T(8,128)S(1)} fusion(f32[8,16,128,128]{3,2,1,0:T(8,128)} %param.5, f32[8,128,16,128]{3,1,2,0:T(8,128)S(1)} %fusion.12, f32[8,16,128,128]{3,2,1,0:T(8,128)} %bitcast.71, pred[8,16]{1,0:T(8,128)(4,1)S(1)} %compare_and_fusion), kind=kOutput, calls=%fused_computation.4 | convolution fusion | flops 3225419776 | bytes 25690240 | tf_op jit(solution)/shard_map/bkuj,bkjr->bur/dot_general | solution.py:16
  588.0 1.0 copy.29
  588.9 0.0 all-reduce.11.cloned.1.call-update
  589.0 0.0 all-reduce.13.cloned.1.call-start
  589.0 137.9 %all-reduce.11.cloned.1.call-done = f32[1024,128]{0,1:T(8,128)} async-done(((f32[1024,128]{0,1:T(8,128)}), f32[1024,128]{0,1:T(8,128)}) %all-reduce.11.cloned.1.call-update) | async-done | bytes 524304 | tf_op jit(solution)/shard_map/psum | solution.py:58
  726.9 1.7 multiply_reduce_fusion.1
  728.7 0.1 multiply_reduce_fusion
  728.8 0.1 multiply_add_fusion.1
  728.9 0.2 copy.30
  729.1 10.3 %fusion.9 = f32[8,128,16,128]{3,1,2,0:T(8,128)S(1)} fusion(f32[8,128,128,1]{2,1,3,0:T(8,128)S(1)} %bitcast.85, f32[8,16,128,128]{3,2,1,0:T(8,128)} %bitcast.72, pred[8,16]{1,0:T(8,128)(4,1)S(1)} %compare_and_fusion), kind=kOutput, calls=%fused_computation.14 | convolution fusion | flops 3223322624 | bytes 17301632 | tf_op jit(solution)/shard_map/bkjr,bur->bkuj/dot_general | solution.py:15
  739.5 12.7 %fusion = f32[8,128,128,1]{2,1,3,0:T(8,128)S(1)} fusion(f32[8,16,128,128]{3,2,1,0:T(8,128)} %param.5, f32[8,128,16,128]{3,1,2,0:T(8,128)S(1)} %fusion.9, f32[8,16,128,128]{3,2,1,0:T(8,128)} %bitcast.73, pred[8,16]{1,0:T(8,128)(4,1)S(1)} %compare_and_fusion), kind=kOutput, calls=%fused_computation.2 | convolution fusion | flops 3225419776 | bytes 25690240 | tf_op jit(solution)/shard_map/bkuj,bkjr->bur/dot_general | solution.py:16
  752.2 1.0 copy.31
  753.2 0.0 all-reduce.13.cloned.1.call-update
  753.2 138.0 %all-reduce.13.cloned.1.call-done = f32[1024,128]{0,1:T(8,128)} async-done(((f32[1024,128]{0,1:T(8,128)}), f32[1024,128]{0,1:T(8,128)}) %all-reduce.13.cloned.1.call-update) | async-done | bytes 524304 | tf_op jit(solution)/shard_map/psum | solution.py:58
  891.2 1.7 fusion.47
  892.9 0.2 multiply_add_fusion
  893.1 1.0 copy.14
  (6 shorter events, 0.0 us)
Async XLA Ops:
  7.4 58.9 %all-gather.3.cloned.1.call-start = ((), (), s32[]{:S(2)}) async-start(), calls=%async_computation.4 | async-start | bytes 2228224 | tf_op jit(solution)/shard_map/all_gather | solution.py:43
  8.1 250.1 %all-reduce.7.cloned.1.call-start = ((), (), s32[]{:S(2)}) async-start(), calls=%async_computation | async-start | bytes 131072 | tf_op jit(solution)/shard_map/psum | solution.py:40
  10.2 387.9 %all-reduce.15.cloned.1.call-start = ((), (), s32[]{:S(2)}) async-start(), calls=%async_computation.5 | async-start | bytes 2097152 | tf_op jit(solution)/shard_map/psum | solution.py:52
  66.2 6.0 copy-start.1
  72.2 11.9 %copy-start = (f32[128,128,128]{2,1,0:T(8,128)S(1)}, f32[128,128,128]{2,1,0:T(8,128)}, u32[]{:S(2)}) copy-start(f32[128,128,128]{2,1,0:T(8,128)} %gather_fusion) | copy-start | bytes 25165828
  109.6 452.9 %all-reduce.9.cloned.1.call-start = ((), (), s32[]{:S(2)}) async-start(), calls=%async_computation.1 | async-start | bytes 1048576 | tf_op jit(solution)/shard_map/psum | solution.py:58
  410.7 151.8 %copy-start.2 = (f32[128,128]{1,0:T(8,128)S(1)}, f32[128,128]{1,0:T(8,128)}, u32[]{:S(2)}) copy-start(f32[128,128]{1,0:T(8,128)} %all-reduce.7.cloned.1.call-done) | copy-start | bytes 196612
  424.5 302.5 %all-reduce.11.cloned.1.call-start = ((), (), s32[]{:S(2)}) async-start(), calls=%async_computation.2 | async-start | bytes 1048576 | tf_op jit(solution)/shard_map/psum | solution.py:58
  589.0 302.2 %all-reduce.13.cloned.1.call-start = ((), (), s32[]{:S(2)}) async-start(), calls=%async_computation.3 | async-start | bytes 1048576 | tf_op jit(solution)/shard_map/psum | solution.py:58
Sparse Core Ops, SparseCore 0:
  10.8 55.3 all-gather.2
Sparse Core Ops, SparseCore 1:
  14.1 244.0 all-reduce.6
  260.7 137.3 all-reduce.14
  424.6 137.8 all-reduce.8
  589.1 137.8 all-reduce.10
  753.3 137.9 all-reduce.12
where the time goes:
time: 909 us; the launch traced here: 902 us
  waiting for transfers between devices  757 us (83%)
  matrix products  114 us (13%)
  between operations  15.4 us (2%)
  local copies, waits for them, and re-layouts  12.8 us (1%)
    psum x3, waiting for transfers between devices, local(): image = lax.psum(partial_image(chosen, weights, direction), 'item')  414 us
    psum x1, waiting for transfers between devices, local(): lax.psum(jnp.dot(slab.T, slab, preferred_element_type=jnp.float32, precis...  148 us
    psum x1, waiting for transfers between devices, local(): rhs, image = lax.psum((rhs_part, start_part), 'item')  140 us
    all_gather x1, waiting for transfers between devices, local(): block = lax.all_gather(slab, 'user', axis=0, tiled=True)  54.6 us
    dot_general x4, matrix products, partial_image(): back = jnp.einsum('bkuj,bkjr->bur', scores * wtiles, chosen, precision=HIGH)  49.7 us
    dot_general x4, matrix products, partial_image(): scores = jnp.einsum('bkjr,bur->bkuj', chosen, shaped, precision=HIGH)  43.3 us
  transfers between devices with their start and end apart: 6, of which 6 were waited for; matrix products, arithmetic and copies ran while one was open for 5% of the time, Pallas kernels for 0%

commit v1 on v0

v1 whole, which is shorter than its diff:
```python
import functools

import jax
import jax.numpy as jnp
from jax import lax
from jax.experimental import pallas as pl
from jax.experimental.pallas import tpu as pltpu
from jax.sharding import PartitionSpec as P

F32 = jnp.float32
BF16 = jnp.bfloat16
MESH = pl.DeviceIdType.MESH

ITERS = 3
ROUNDS = ITERS + 1
PERIOD = 12
AT_SUM = 2
AT_SOLVE = 6
AT_SPREAD = 10

NX, NYH, NCORE = 4, 2, 2
NZ, NYL = 8, 2


def split(value):
    high = value.astype(BF16)
    low = (value - high.astype(F32)).astype(BF16)
    return high, low


def kernel(
    blocks,
    count,
    ids_ref,
    weights_hbm,
    slab_ref,
    start_hbm,
    out_hbm,
    weights_ref,
    vbuf,
    vcat,
    gram_acc,
    gram_cat,
    direct,
    part,
    ybuf,
    zsum,
    zbuf,
    xs,
    rs,
    ps,
    norms,
    local_sem,
    out_sem,
    g_send,
    g_recv,
    y_send,
    y_recv,
    z_send,
    z_recv,
    a_send,
    a_recv,
    b_send,
    b_recv,
):
    user = lax.axis_index("user")
    item = lax.axis_index("item")
    tile = direct.shape[1]
    half = tile // NYL
    piece = half // NZ
    rows = slab_ref.shape[0]

    load_w = pltpu.make_async_copy(weights_hbm, weights_ref, local_sem.at[0])
    load_w.start()
    load_x = pltpu.make_async_copy(start_hbm, direct, local_sem.at[1])
    load_x.start()

    px, pyh, pc = user // (NYH * NCORE), lax.rem(user // NCORE, NYH), lax.rem(user, NCORE)
    pz, pyl = item // NYL, lax.rem(item, NYL)

    def uslot(x, yh, c):
        return x * (NYH * NCORE) + yh * NCORE + c

    xl, xr, xo = lax.rem(px + 3, NX), lax.rem(px + 1, NX), lax.rem(px + 2, NX)
    qyh, qc = 1 - pyh, 1 - pc
    dev_y = (uslot(px, qyh, pc), item)
    dev_l = (uslot(xl, pyh, pc), item)
    dev_r = (uslot(xr, pyh, pc), item)
    dev_c = (uslot(px, pyh, qc), item)
    dev_p = (user, pz * NYL + (1 - pyl))

    def dev_z(rel):
        return (user, lax.rem(pz + rel, NZ) * NYL + pyl)

    barrier = pltpu.get_barrier_semaphore()
    greeted = [dev_y, dev_l, dev_r, dev_c, dev_p] + [dev_z(rel) for rel in range(1, NZ)]
    for dev in greeted:
        pl.semaphore_signal(barrier, inc=1, device_id=dev, device_id_type=MESH)
    pl.semaphore_wait(barrier, len(greeted))

    sends = []

    def send(src, slot, lo, n, dev, sem):
        copy = pltpu.make_async_remote_copy(
            src_ref=src.at[pl.ds(lo, n)],
            dst_ref=vbuf.at[slot, pl.ds(lo, n)],
            send_sem=g_send.at[sem],
            recv_sem=g_recv.at[sem],
            device_id=dev,
            device_id_type=MESH,
        )
        copy.start()
        sends.append(copy)

    def arrived(slot, lo, n, sem):
        view = vbuf.at[slot, pl.ds(lo, n)]
        pltpu.make_async_copy(view, view, g_recv.at[sem]).wait()

    gram_acc[...] = jnp.zeros_like(gram_acc)

    def convert(src, slot):
        for j in range(rows // tile):
            high, low = split(src[pl.ds(j * tile, tile), :])
            cat = jnp.concatenate([high, low], axis=1)
            vcat[slot * (rows // tile) + j] = cat
            gram_acc[...] += lax.dot_general(
                cat, cat, (((0,), (0,)), ((), ())), preferred_element_type=F32
            )

    own = uslot(px, pyh, pc)
    HB = rows // 2
    Y, L0, R0, L1, R1, O0A, O0B, O1A, O1B, C0 = 0, 1, 2, 3, 4, 5, 6, 7, 8, 9
    send(slab_ref, own, 0, rows, dev_y, Y)
    send(slab_ref, own, 0, rows, dev_r, L0)
    send(slab_ref, own, 0, rows, dev_l, R0)
    send(slab_ref, own, 0, rows, dev_c, C0)
    convert(slab_ref, own)

    def take(slot, sem, right, left, core):
        arrived(slot, 0, rows, sem)
        if right is not None:
            send(vbuf.at[slot], slot, 0, right[1], dev_r, right[0])
        if left is not None:
            send(vbuf.at[slot], slot, rows - left[1], left[1], dev_l, left[0])
        send(vbuf.at[slot], slot, 0, rows, dev_c, core)

    take(uslot(xl, pyh, pc), L0, (O0A, HB), None, C0 + 2)
    take(uslot(xr, pyh, pc), R0, None, (O0B, HB), C0 + 3)
    convert(vbuf.at[uslot(xl, pyh, pc)], uslot(xl, pyh, pc))
    take(uslot(px, qyh, pc), Y, (L1, rows), (R1, rows), C0 + 1)
    convert(vbuf.at[uslot(xr, pyh, pc)], uslot(xr, pyh, pc))
    convert(vbuf.at[uslot(px, qyh, pc)], uslot(px, qyh, pc))
    near = uslot(xo, pyh, pc)
    arrived(near, 0, HB, O0A)
    arrived(near, HB, HB, O0B)
    send(vbuf.at[near], near, 0, rows, dev_c, C0 + 6)
    convert(vbuf.at[near], near)
    take(uslot(xl, qyh, pc), L1, (O1A, HB), None, C0 + 4)
    take(uslot(xr, qyh, pc), R1, None, (O1B, HB), C0 + 5)
    convert(vbuf.at[uslot(xl, qyh, pc)], uslot(xl, qyh, pc))
    convert(vbuf.at[uslot(xr, qyh, pc)], uslot(xr, qyh, pc))
    cores = [
        (uslot(px, pyh, qc), C0),
        (uslot(xl, pyh, qc), C0 + 2),
        (uslot(xr, pyh, qc), C0 + 3),
        (uslot(px, qyh, qc), C0 + 1),
        (uslot(xo, pyh, qc), C0 + 6),
        (uslot(xl, qyh, qc), C0 + 4),
        (uslot(xr, qyh, qc), C0 + 5),
    ]
    for slot, sem in cores[:5]:
        arrived(slot, 0, rows, sem)
        convert(vbuf.at[slot], slot)
    far = uslot(xo, qyh, pc)
    arrived(far, 0, HB, O1A)
    arrived(far, HB, HB, O1B)
    send(vbuf.at[far], far, 0, rows, dev_c, C0 + 7)
    convert(vbuf.at[far], far)
    for slot, sem in cores[5:] + [(uslot(xo, qyh, qc), C0 + 7)]:
        arrived(slot, 0, rows, sem)
        convert(vbuf.at[slot], slot)
    for copy in sends:
        copy.wait_send()

    gram = gram_acc[...]
    gram = gram[:tile] + gram[tile:]
    gram = gram[:, :tile] + gram[:, tile:]
    gram_cat[...] = jnp.concatenate(split(gram), axis=1)

    load_x.wait()
    load_w.wait()

    def image(c, first):
        vec = direct[c]
        if first:
            vec = -vec
        high, low = split(vec)
        lhs = jnp.concatenate(
            [jnp.concatenate([high, high], axis=1), jnp.concatenate([low, low], axis=1)], axis=0
        )
        acc = jnp.dot(
            jnp.concatenate([high, low], axis=0), gram_cat[...], preferred_element_type=F32
        )
        for k in range(0, count, 2):
            base = c * count + k
            pair = jnp.concatenate([vcat[ids_ref[base]], vcat[ids_ref[base + 1]]], axis=0)
            scores = lax.dot_general(
                lhs, pair, (((1,), (1,)), ((), ())), preferred_element_type=F32
            )
            scores = scores[:tile] + scores[tile:]
            wt = jnp.concatenate([weights_ref[base], weights_ref[base + 1]], axis=1)
            scaled = scores * wt
            if first:
                scaled = scaled + jnp.where(wt > 0, 1.0 + wt, 0.0)
            acc += jnp.dot(
                jnp.concatenate(split(scaled), axis=0), pair, preferred_element_type=F32
            )
        acc = acc[:tile] + acc[tile:]
        part[c] = acc[:, :tile] + acc[:, tile:]

    mine = pl.multiple_of(pyl * half, half)
    other = pl.multiple_of((1 - pyl) * half, half)
    zrow = pl.multiple_of(pz * piece, piece)
    prow = pl.multiple_of(pyl * half + pz * piece, piece)

    def copy_y(c):
        return pltpu.make_async_remote_copy(
            src_ref=part.at[c, pl.ds(other, half)],
            dst_ref=ybuf.at[c],
            send_sem=y_send.at[c],
            recv_sem=y_recv.at[c],
            device_id=dev_p,
            device_id_type=MESH,
        )

    def copy_b(c):
        return pltpu.make_async_remote_copy(
            src_ref=direct.at[c, pl.ds(mine, half)],
            dst_ref=direct.at[c, pl.ds(mine, half)],
            send_sem=b_send.at[c],
            recv_sem=b_recv.at[c],
            device_id=dev_p,
            device_id_type=MESH,
        )

    def wait_all(c, sem):
        view = zbuf.at[c]
        pltpu.make_async_copy(view, view, sem.at[c]).wait()

    def stage_image(c, t):
        @pl.when(t > 0)
        def _():
            copy_b(c).wait()

        @pl.when(t == 0)
        def _():
            image(c, True)

        @pl.when(jnp.logical_and(t > 0, t < ROUNDS))
        def _():
            image(c, False)

        @pl.when(t < ROUNDS)
        def _():
            copy_y(c).start()

        @pl.when(t == ROUNDS)
        def _():
            pltpu.make_async_copy(direct.at[c], out_hbm.at[c], out_sem.at[c]).start()

    def stage_sum(c):
        copy_y(c).wait()
        zsum[c] = part[c, pl.ds(mine, half), :] + ybuf[c]
        for rel in range(1, NZ):
            row = pl.multiple_of(lax.rem(pz + rel, NZ) * piece, piece)
            pltpu.make_async_remote_copy(
                src_ref=zsum.at[c, pl.ds(row, piece)],
                dst_ref=zbuf.at[c, NZ - 1 - rel],
                send_sem=z_send.at[c],
                recv_sem=z_recv.at[c],
                device_id=dev_z(rel),
                device_id_type=MESH,
            ).start()

    def spread(c):
        for rel in range(1, NZ):
            pltpu.make_async_remote_copy(
                src_ref=direct.at[c, pl.ds(prow, piece)],
                dst_ref=direct.at[c, pl.ds(prow, piece)],
                send_sem=a_send.at[c],
                recv_sem=a_recv.at[c],
                device_id=dev_z(rel),
                device_id_type=MESH,
            ).start()

    def stage_solve(c, t):
        wait_all(c, z_send)
        wait_all(c, z_recv)
        got = zsum[c, pl.ds(zrow, piece), :]
        for k in range(NZ - 1):
            got = got + zbuf[c, k]

        @pl.when(t == 0)
        def _():
            x0 = direct[c, pl.ds(prow, piece), :]
            r = got - 1.0 * x0
            xs[c] = x0
            rs[c] = r
            ps[c] = r
            norms[c] = jnp.broadcast_to(jnp.sum(r * r, axis=1, keepdims=True), r.shape)
            direct[c, pl.ds(prow, piece), :] = r

        @pl.when(t > 0)
        def _():
            p = ps[c]
            q = got + 1.0 * p
            now = norms[c]
            alpha = now / (jnp.sum(p * q, axis=1, keepdims=True) + 1e-06)
            x = xs[c] + alpha * p
            r = rs[c] - alpha * q
            after = jnp.broadcast_to(jnp.sum(r * r, axis=1, keepdims=True), r.shape)
            p = r + after / (now + 1e-06) * p
            xs[c] = x
            rs[c] = r
            ps[c] = p
            norms[c] = after
            direct[c, pl.ds(prow, piece), :] = jnp.where(t == ROUNDS - 1, x, p)

        spread(c)

    def stage_spread(c):
        wait_all(c, a_send)
        wait_all(c, a_recv)
        copy_b(c).start()

    def guarded(step, offset, rounds, body):
        at = step - offset
        t = lax.div(at, PERIOD)
        c = lax.rem(at, PERIOD)

        @pl.when(jnp.logical_and(at >= 0, jnp.logical_and(t < rounds, c < blocks)))
        def _():
            body(c, t)

    def step_body(step, carry):
        guarded(step, AT_SPREAD, ROUNDS, lambda c, t: stage_spread(c))
        guarded(step, AT_SOLVE, ROUNDS, stage_solve)
        guarded(step, AT_SUM, ROUNDS, lambda c, t: stage_sum(c))
        guarded(step, 0, ROUNDS + 1, stage_image)
        return carry

    lax.fori_loop(0, ROUNDS * PERIOD + blocks, step_body, 0)
    for c in range(blocks):
        pltpu.make_async_copy(direct.at[c], out_hbm.at[c], out_sem.at[c]).wait()


def local(item_factors, weights, tile_ids, start_factors):
    blocks, count, tile, _ = weights.shape
    _, rows, rank = item_factors.shape
    gathered = NX * NYH * NCORE
    half = tile // NYL
    piece = half // NZ
    dma = pltpu.SemaphoreType.DMA
    vmem = pltpu.VMEM
    out = pl.pallas_call(
        functools.partial(kernel, blocks, count),
        out_shape=jax.ShapeDtypeStruct((blocks, tile, rank), F32),
        in_specs=[
            pl.BlockSpec(memory_space=pltpu.SMEM),
            pl.BlockSpec(memory_space=pl.ANY),
            pl.BlockSpec(memory_space=vmem),
            pl.BlockSpec(memory_space=pl.ANY),
        ],
        out_specs=pl.BlockSpec(memory_space=pl.ANY),
        scratch_shapes=[
            vmem((blocks * count, tile, tile), F32),
            vmem((gathered, rows, rank), F32),
            vmem((gathered * rows // tile, tile, 2 * rank), BF16),
            vmem((2 * rank, 2 * rank), F32),
            vmem((rank, 2 * rank), BF16),
            vmem((blocks, tile, rank), F32),
            vmem((blocks, tile, rank), F32),
            vmem((blocks, half, rank), F32),
            vmem((blocks, half, rank), F32),
            vmem((blocks, NZ - 1, piece, rank), F32),
            vmem((blocks, piece, rank), F32),
            vmem((blocks, piece, rank), F32),
            vmem((blocks, piece, rank), F32),
            vmem((blocks, piece, rank), F32),
            dma((2,)),
            dma((blocks,)),
            dma((17,)),
            dma((17,)),
        ]
        + [dma((blocks,))] * 8,
        compiler_params=pltpu.CompilerParams(collective_id=0, has_side_effects=True),
        name="als_sweep",
    )(
        tile_ids.reshape(blocks * count),
        weights.reshape(blocks * count, tile, tile),
        item_factors.reshape(rows, rank),
        start_factors.reshape(blocks, tile, rank),
    )
    return out.reshape(blocks * tile, rank)


def solution(mesh):
    in_specs = (
        P("item", "user", None),
        P("user", "item", None, None),
        P("user", "item", None),
        P("user", None),
    )
    out_specs = P("user", None)
    return jax.shard_map(local, mesh=mesh, in_specs=in_specs, out_specs=out_specs, check_vma=False)
```

time: 909 us -> 123 us (0.14)
  waiting for transfers between devices: 757 us -> 0 us
  Pallas kernels: 0 us -> 118 us
  matrix products: 114 us -> 0 us
  between operations: 15.4 us -> 0.01 us
  local copies, waits for them, and re-layouts: 12.8 us -> 2.97 us
    psum x5 -> x0, waiting for transfers between devices: 702 us -> none  [the longest x3 414 us: local(): image = lax.psum(partial_image(chosen, weights, direction), 'item')]
    pallas_call x0 -> x1, Pallas kernels: none -> 118 us  [local(): pl.pallas_call(functools.partial(kernel, blocks, count), out_shape=jax.Sh...]
    dot_general x14 -> x0, matrix products: 114 us -> none  [the longest x4 49.7 us: partial_image(): back = jnp.einsum('bkuj,bkjr->bur', scores * wtiles, chosen, precision=HIGH)]
    all_gather x1 -> x0, waiting for transfers between devices: 54.6 us -> none  [local(): block = lax.all_gather(slab, 'user', axis=0, tiled=True)]
  transfers between devices with their start and end apart: 6 -> 0, of which waited for: 6 -> 0; matrix products, arithmetic and copies ran while one was open for 5% -> 0% of each run, Pallas kernels for 0% -> 0%
where the time goes in v1:
time: 123 us; the launch traced here: 122 us
  Pallas kernels  118 us (96%)
  local copies, waits for them, and re-layouts  2.97 us (2%)
  other arithmetic  1.35 us (1%)
    pallas_call x1, Pallas kernels, local(): pl.pallas_call(functools.partial(kernel, blocks, count), out_shape=jax.Sh...  118 us

profile of v1, /device:TPU:8, one launch (start us, length us, event | category | flops | bytes accessed | tf_op | source)
XLA Modules:
  0.0 122.4 jit_solution(12421573760268051018)
XLA Ops:
  0.0 0.5 broadcast.3
  0.5 1.3 %reduce.3 = s32[8,16]{1,0:T(8,128)S(1)} reduce(s32[8,1,16]{2,1,0:T(1,128)} %param.6, s32[]{:T(128)} %broadcast.3), dimensions={1}, to_apply=%param.6.reduce_sub_computation.3 | reduce | bytes 1028 | tf_op args[2]
  1.9 0.6 reshape.15.ids_ref
  2.5 118.0 %als_sweep.1 = f32[8,128,128]{2,1,0:T(8,128)} custom-call(s32[128]{0:T(128)} %reshape.15.ids_ref, f32[128,128,128]{2,1,0:T(8,128)} %bitcast.4, f32[256,128]{1,0:T(8,128)} %bitcast.7, f32[8,128,128]{2,1,0:T(8,128)} %bitcast.6), custom_call_target="tpu_custom_call" | custom-call | tf_op jit(solution)/shard_map/als_sweep/pallas_call | solution.py:365
  120.5 1.9 %copy.6 = f32[1024,128]{1,0:T(8,128)} copy(f32[1024,128]{1,0:T(8,128)} %bitcast.5) | data formatting | bytes 1048576

commit v2 on v1

--- a/solution.py
+++ b/solution.py
@@ -13,10 +13,12 @@
 
 ITERS = 3
 ROUNDS = ITERS + 1
-PERIOD = 12
+PERIOD = 11
 AT_SUM = 2
-AT_SOLVE = 6
-AT_SPREAD = 10
+AT_SOLVE = 5
+AT_SPREAD = 8
+RS_ALL = False
+AG_ALL = False
 
 NX, NYH, NCORE = 4, 2, 2
 NZ, NYL = 8, 2
@@ -86,99 +88,102 @@
     dev_y = (uslot(px, qyh, pc), item)
     dev_l = (uslot(xl, pyh, pc), item)
     dev_r = (uslot(xr, pyh, pc), item)
+    dev_o = (uslot(xo, pyh, pc), item)
     dev_c = (uslot(px, pyh, qc), item)
     dev_p = (user, pz * NYL + (1 - pyl))
 
-    def dev_z(rel):
-        return (user, lax.rem(pz + rel, NZ) * NYL + pyl)
+    peers = [(dz, dy) for dz in (4, 3, 5, 2, 6, 1, 7, 0) for dy in (1, 0) if dz or dy]
+    column = [(dz, dy) for dz, dy in peers if dy == 0]
+    rs_peers = peers if RS_ALL else column
+    ag_peers = peers if AG_ALL else column
+
+    def place(dz, dy):
+        return lax.rem(pz + dz, NZ), lax.rem(pyl + dy, NYL)
+
+    def dev_z(dz, dy):
+        z, y = place(dz, dy)
+        return (user, z * NYL + y)
+
+    def slot_of(dz, dy, group):
+        return group.index(((NZ - dz) % NZ, dy))
 
     barrier = pltpu.get_barrier_semaphore()
-    greeted = [dev_y, dev_l, dev_r, dev_c, dev_p] + [dev_z(rel) for rel in range(1, NZ)]
+    greeted = [dev_y, dev_l, dev_r, dev_o, dev_c] + [dev_z(dz, dy) for dz, dy in peers]
     for dev in greeted:
         pl.semaphore_signal(barrier, inc=1, device_id=dev, device_id_type=MESH)
     pl.semaphore_wait(barrier, len(greeted))
 
+    parts = rows // tile
     sends = []
 
-    def send(src, slot, lo, n, dev, sem):
+    def send(src, slot, j, dev, kind):
         copy = pltpu.make_async_remote_copy(
-            src_ref=src.at[pl.ds(lo, n)],
-            dst_ref=vbuf.at[slot, pl.ds(lo, n)],
-            send_sem=g_send.at[sem],
-            recv_sem=g_recv.at[sem],
+            src_ref=src.at[pl.ds(j * tile, tile)],
+            dst_ref=vbuf.at[slot, pl.ds(j * tile, tile)],
+            send_sem=g_send.at[kind * parts + j],
+            recv_sem=g_recv.at[kind * parts + j],
             device_id=dev,
             device_id_type=MESH,
         )
         copy.start()
         sends.append(copy)
 
-    def arrived(slot, lo, n, sem):
-        view = vbuf.at[slot, pl.ds(lo, n)]
-        pltpu.make_async_copy(view, view, g_recv.at[sem]).wait()
+    def arrived(slot, j, kind):
+        view = vbuf.at[slot, pl.ds(j * tile, tile)]
+        pltpu.make_async_copy(view, view, g_recv.at[kind * parts + j]).wait()
 
     gram_acc[...] = jnp.zeros_like(gram_acc)
 
-    def convert(src, slot):
-        for j in range(rows // tile):
-            high, low = split(src[pl.ds(j * tile, tile), :])
-            cat = jnp.concatenate([high, low], axis=1)
-            vcat[slot * (rows // tile) + j] = cat
-            gram_acc[...] += lax.dot_general(
-                cat, cat, (((0,), (0,)), ((), ())), preferred_element_type=F32
-            )
+    def convert(src, slot, j):
+        high, low = split(src[pl.ds(j * tile, tile), :])
+        cat = jnp.concatenate([high, low], axis=1)
+        vcat[slot * parts + j] = cat
+        gram_acc[...] += lax.dot_general(
+            cat, cat, (((0,), (0,)), ((), ())), preferred_element_type=F32
+        )
 
     own = uslot(px, pyh, pc)
-    HB = rows // 2
-    Y, L0, R0, L1, R1, O0A, O0B, O1A, O1B, C0 = 0, 1, 2, 3, 4, 5, 6, 7, 8, 9
-    send(slab_ref, own, 0, rows, dev_y, Y)
-    send(slab_ref, own, 0, rows, dev_r, L0)
-    send(slab_ref, own, 0, rows, dev_l, R0)
-    send(slab_ref, own, 0, rows, dev_c, C0)
-    convert(slab_ref, own)
-
-    def take(slot, sem, right, left, core):
-        arrived(slot, 0, rows, sem)
-        if right is not None:
-            send(vbuf.at[slot], slot, 0, right[1], dev_r, right[0])
-        if left is not None:
-            send(vbuf.at[slot], slot, rows - left[1], left[1], dev_l, left[0])
-        send(vbuf.at[slot], slot, 0, rows, dev_c, core)
-
-    take(uslot(xl, pyh, pc), L0, (O0A, HB), None, C0 + 2)
-    take(uslot(xr, pyh, pc), R0, None, (O0B, HB), C0 + 3)
-    convert(vbuf.at[uslot(xl, pyh, pc)], uslot(xl, pyh, pc))
-    take(uslot(px, qyh, pc), Y, (L1, rows), (R1, rows), C0 + 1)
-    convert(vbuf.at[uslot(xr, pyh, pc)], uslot(xr, pyh, pc))
-    convert(vbuf.at[uslot(px, qyh, pc)], uslot(px, qyh, pc))
-    near = uslot(xo, pyh, pc)
-    arrived(near, 0, HB, O0A)
-    arrived(near, HB, HB, O0B)
-    send(vbuf.at[near], near, 0, rows, dev_c, C0 + 6)
-    convert(vbuf.at[near], near)
-    take(uslot(xl, qyh, pc), L1, (O1A, HB), None, C0 + 4)
-    take(uslot(xr, qyh, pc), R1, None, (O1B, HB), C0 + 5)
-    convert(vbuf.at[uslot(xl, qyh, pc)], uslot(xl, qyh, pc))
-    convert(vbuf.at[uslot(xr, qyh, pc)], uslot(xr, qyh, pc))
-    cores = [
-        (uslot(px, pyh, qc), C0),
-        (uslot(xl, pyh, qc), C0 + 2),
-        (uslot(xr, pyh, qc), C0 + 3),
-        (uslot(px, qyh, qc), C0 + 1),
-        (uslot(xo, pyh, qc), C0 + 6),
-        (uslot(xl, qyh, qc), C0 + 4),
-        (uslot(xr, qyh, qc), C0 + 5),
-    ]
-    for slot, sem in cores[:5]:
-        arrived(slot, 0, rows, sem)
-        convert(vbuf.at[slot], slot)
-    far = uslot(xo, qyh, pc)
-    arrived(far, 0, HB, O1A)
-    arrived(far, HB, HB, O1B)
-    send(vbuf.at[far], far, 0, rows, dev_c, C0 + 7)
-    convert(vbuf.at[far], far)
-    for slot, sem in cores[5:] + [(uslot(xo, qyh, qc), C0 + 7)]:
-        arrived(slot, 0, rows, sem)
-        convert(vbuf.at[slot], slot)
+    Y, L0, R0, O0, L1, R1, O1, C0 = range(8)
+    for j in range(parts):
+        send(slab_ref, own, j, dev_y, Y)
+        send(slab_ref, own, j, dev_r, L0)
+        send(slab_ref, own, j, dev_l, R0)
+        send(slab_ref, own, j, dev_o, O0)
+        send(slab_ref, own, j, dev_c, C0)
+    for j in range(parts):
+        convert(slab_ref, own, j)
+    across = uslot(px, qyh, pc)
+    for j in range(parts):
+        arrived(across, j, Y)
+        send(vbuf.at[across], across, j, dev_r, L1)
+        send(vbuf.at[across], across, j, dev_l, R1)
+        send(vbuf.at[across], across, j, dev_o, O1)
+        send(vbuf.at[across], across, j, dev_c, C0 + Y + 1)
+    routes = [(xl, pyh, L0), (xr, pyh, R0), (xo, pyh, O0), (xl, qyh, L1), (xr, qyh, R1), (xo, qyh, O1)]
+    for x, yh, kind in routes[:3]:
+        for j in range(parts):
+            slot = uslot(x, yh, pc)
+            arrived(slot, j, kind)
+            send(vbuf.at[slot], slot, j, dev_c, C0 + kind + 1)
+    for x, yh, kind in [(px, qyh, Y)] + routes[:3]:
+        for j in range(parts):
+            convert(vbuf.at[uslot(x, yh, pc)], uslot(x, yh, pc), j)
+    for x, yh, kind in [(px, pyh, -1), (px, qyh, Y)] + routes[:3]:
+        for j in range(parts):
+            slot = uslot(x, yh, qc)
+            arrived(slot, j, C0 + kind + 1)
+            convert(vbuf.at[slot], slot, j)
+    for j in range(parts):
+        for x, yh, kind in routes[3:]:
+            slot = uslot(x, yh, pc)
+            arrived(slot, j, kind)
+            send(vbuf.at[slot], slot, j, dev_c, C0 + kind + 1)
+            convert(vbuf.at[slot], slot, j)
+    for j in range(parts):
+        for x, yh, kind in routes[3:]:
+            slot = uslot(x, yh, qc)
+            arrived(slot, j, C0 + kind + 1)
+            convert(vbuf.at[slot], slot, j)
     for copy in sends:
         copy.wait_send()
 
@@ -203,7 +208,7 @@
         )
         for k in range(0, count, 2):
             base = c * count + k
-            pair = jnp.concatenate([vcat[ids_ref[base]], vcat[ids_ref[base + 1]]], axis=0)
+            pair = jnp.concatenate([vcat[ids_ref[c, 0, k]], vcat[ids_ref[c, 0, k + 1]]], axis=0)
             scores = lax.dot_general(
                 lhs, pair, (((1,), (1,)), ((), ())), preferred_element_type=F32
             )
@@ -243,14 +248,31 @@
             device_id_type=MESH,
         )
 
-    def wait_all(c, sem):
-        view = zbuf.at[c]
+    def wait_all(c, sem, n):
+        view = zbuf.at[c, pl.ds(0, n)]
         pltpu.make_async_copy(view, view, sem.at[c]).wait()
+
+    def scatter(src, c):
+        for dz, dy in rs_peers:
+            z, y = place(dz, dy)
+            row = z * piece + (y * half if RS_ALL else 0)
+            pltpu.make_async_remote_copy(
+                src_ref=src.at[c, pl.ds(pl.multiple_of(row, piece), piece)],
+                dst_ref=zbuf.at[c, slot_of(dz, dy, rs_peers)],
+                send_sem=z_send.at[c],
+                recv_sem=z_recv.at[c],
+                device_id=dev_z(dz, dy),
+                device_id_type=MESH,
+            ).start()
 
     def stage_image(c, t):
         @pl.when(t > 0)
         def _():
-            copy_b(c).wait()
+            if AG_ALL:
+                wait_all(c, a_send, len(ag_peers))
+                wait_all(c, a_recv, len(ag_peers))
+            else:
+                copy_b(c).wait()
 
         @pl.when(t == 0)
         def _():
@@ -262,7 +284,10 @@
 
         @pl.when(t < ROUNDS)
         def _():
-            copy_y(c).start()
+            if RS_ALL:
+                scatter(part, c)
+            else:
+                copy_y(c).start()
 
         @pl.when(t == ROUNDS)
         def _():
@@ -271,33 +296,24 @@
     def stage_sum(c):
         copy_y(c).wait()
         zsum[c] = part[c, pl.ds(mine, half), :] + ybuf[c]
-        for rel in range(1, NZ):
-            row = pl.multiple_of(lax.rem(pz + rel, NZ) * piece, piece)
-            pltpu.make_async_remote_copy(
-                src_ref=zsum.at[c, pl.ds(row, piece)],
-                dst_ref=zbuf.at[c, NZ - 1 - rel],
-                send_sem=z_send.at[c],
-                recv_sem=z_recv.at[c],
-                device_id=dev_z(rel),
-                device_id_type=MESH,
-            ).start()
+        scatter(zsum, c)
 
     def spread(c):
-        for rel in range(1, NZ):
+        for dz, dy in ag_peers:
             pltpu.make_async_remote_copy(
                 src_ref=direct.at[c, pl.ds(prow, piece)],
                 dst_ref=direct.at[c, pl.ds(prow, piece)],
                 send_sem=a_send.at[c],
                 recv_sem=a_recv.at[c],
-                device_id=dev_z(rel),
+                device_id=dev_z(dz, dy),
                 device_id_type=MESH,
             ).start()
 
     def stage_solve(c, t):
-        wait_all(c, z_send)
-        wait_all(c, z_recv)
-        got = zsum[c, pl.ds(zrow, piece), :]
-        for k in range(NZ - 1):
+        wait_all(c, z_send, len(rs_peers))
+        wait_all(c, z_recv, len(rs_peers))
+        got = part[c, pl.ds(prow, piece), :] if RS_ALL else zsum[c, pl.ds(zrow, piece), :]
+        for k in range(len(rs_peers)):
             got = got + zbuf[c, k]
 
         @pl.when(t == 0)
@@ -329,8 +345,8 @@
         spread(c)
 
     def stage_spread(c):
-        wait_all(c, a_send)
-        wait_all(c, a_recv)
+        wait_all(c, a_send, len(ag_peers))
+        wait_all(c, a_recv, len(ag_peers))
         copy_b(c).start()
 
     def guarded(step, offset, rounds, body):
@@ -343,10 +359,12 @@
             body(c, t)
 
     def step_body(step, carry):
-        guarded(step, AT_SPREAD, ROUNDS, lambda c, t: stage_spread(c))
+        guarded(step, 0, ROUNDS + 1, stage_image)
+        if not RS_ALL:
+            guarded(step, AT_SUM, ROUNDS, lambda c, t: stage_sum(c))
         guarded(step, AT_SOLVE, ROUNDS, stage_solve)
-        guarded(step, AT_SUM, ROUNDS, lambda c, t: stage_sum(c))
-        guarded(step, 0, ROUNDS + 1, stage_image)
+        if not AG_ALL:
+            guarded(step, AT_SPREAD, ROUNDS, lambda c, t: stage_spread(c))
         return carry
 
     lax.fori_loop(0, ROUNDS * PERIOD + blocks, step_body, 0)
@@ -382,21 +400,21 @@
             vmem((blocks, tile, rank), F32),
             vmem((blocks, half, rank), F32),
             vmem((blocks, half, rank), F32),
-            vmem((blocks, NZ - 1, piece, rank), F32),
+            vmem((blocks, NZ * NYL - 1, piece, rank), F32),
             vmem((blocks, piece, rank), F32),
             vmem((blocks, piece, rank), F32),
             vmem((blocks, piece, rank), F32),
             vmem((blocks, piece, rank), F32),
             dma((2,)),
             dma((blocks,)),
-            dma((17,)),
-            dma((17,)),
+            dma((15 * rows // tile,)),
+            dma((15 * rows // tile,)),
         ]
         + [dma((blocks,))] * 8,
         compiler_params=pltpu.CompilerParams(collective_id=0, has_side_effects=True),
         name="als_sweep",
     )(
-        tile_ids.reshape(blocks * count),
+        tile_ids,
         weights.reshape(blocks * count, tile, tile),
         item_factors.reshape(rows, rank),
         start_factors.reshape(blocks, tile, rank),

time: 123 us -> 105 us (0.85)
  Pallas kernels: 118 us -> 103 us
  other arithmetic: 1.35 us -> 0 us
    pallas_call x1, Pallas kernels: 118 us -> 103 us  [local(): pl.pallas_call(functools.partial(kernel, blocks, count), out_shape=jax.Sh...]
    unnamed x1 -> x0, other arithmetic: 1.35 us -> none
where the time goes in v2:
time: 105 us
  Pallas kernels  103 us (98%)
  local copies, waits for them, and re-layouts  1.87 us (2%)
    pallas_call x1, Pallas kernels, local(): pl.pallas_call(functools.partial(kernel, blocks, count), out_shape=jax.Sh...  103 us

profile of v2, /device:TPU:8, one launch (start us, length us, event | category | flops | bytes accessed | tf_op | source)
XLA Modules:
  0.0 104.9 jit_solution(4181850595823277939)
XLA Ops:
  0.0 103.0 %als_sweep.1 = f32[8,128,128]{2,1,0:T(8,128)} custom-call(s32[8,1,16]{2,1,0:T(1,128)} %ids_ref.1, f32[128,128,128]{2,1,0:T(8,128)} %bitcast.4, f32[256,128]{1,0:T(8,128)} %bitcast.7, f32[8,128,128]{2,1,0:T(8,128)} %bitcast.6), custom_call_target="tpu_custom_call" | custom-call | tf_op jit(solution)/shard_map/als_sweep/pallas_call | solution.py:383
  103.0 1.9 %copy.6 = f32[1024,128]{1,0:T(8,128)} copy(f32[1024,128]{1,0:T(8,128)} %bitcast.5) | data formatting | bytes 1048576

commit v3 on v2

v3 whole, which is shorter than its diff:
```python
import functools

import jax
import jax.numpy as jnp
from jax import lax
from jax.experimental import pallas as pl
from jax.experimental.pallas import tpu as pltpu
from jax.sharding import PartitionSpec as P

F32 = jnp.float32
BF16 = jnp.bfloat16
MESH = pl.DeviceIdType.MESH

ITERS = 3
ROUNDS = ITERS
PERIOD = 11
AT_SUM = 2
AT_SOLVE = 5
AT_SPREAD = 8
AT_LAST = 6

NX, NYH, NCORE = 4, 2, 2
NZ, NYL = 8, 2


def split(value):
    high = value.astype(BF16)
    low = (value - high.astype(F32)).astype(BF16)
    return high, low


def kernel(
    blocks,
    count,
    ids_hbm,
    weights_hbm,
    slab_hbm,
    start_hbm,
    out_hbm,
    ids_ref,
    weights_ref,
    vbuf,
    vcat,
    gram_acc,
    gram_cat,
    direct,
    part,
    ybuf,
    zsum,
    zbuf,
    scal,
    dots,
    rs,
    ps,
    norms,
    alphas,
    local_sem,
    out_sem,
    g_send,
    g_recv,
    y_send,
    y_recv,
    z_send,
    z_recv,
    a_send,
    a_recv,
    b_send,
    b_recv,
    s_send,
    s_recv,
    e_send,
    e_recv,
    d_send,
    d_recv,
):
    user = lax.axis_index("user")
    item = lax.axis_index("item")
    tile = direct.shape[2]
    half = tile // NYL
    piece = half // NZ
    rows = vbuf.shape[1]

    px, pyh, pc = user // (NYH * NCORE), lax.rem(user // NCORE, NYH), lax.rem(user, NCORE)
    pz, pyl = item // NYL, lax.rem(item, NYL)

    def uslot(x, yh, c):
        return x * (NYH * NCORE) + yh * NCORE + c

    xl, xr, xo = lax.rem(px + 3, NX), lax.rem(px + 1, NX), lax.rem(px + 2, NX)
    qyh, qc = 1 - pyh, 1 - pc
    dev_y = (uslot(px, qyh, pc), item)
    dev_l = (uslot(xl, pyh, pc), item)
    dev_r = (uslot(xr, pyh, pc), item)
    dev_o = (uslot(xo, pyh, pc), item)
    dev_c = (uslot(px, pyh, qc), item)
    dev_p = (user, pz * NYL + (1 - pyl))

    peers = [(dz, dy) for dz in (4, 3, 5, 2, 6, 1, 7, 0) for dy in (1, 0) if dz or dy]
    column = [(dz, dy) for dz, dy in peers if dy == 0]

    def place(dz, dy):
        return lax.rem(pz + dz, NZ), lax.rem(pyl + dy, NYL)

    def dev_z(dz, dy):
        z, y = place(dz, dy)
        return (user, z * NYL + y)

    def slot_of(dz):
        return column.index((NZ - dz, 0))

    barrier = pltpu.get_barrier_semaphore()
    greeted = [dev_y, dev_l, dev_r, dev_o, dev_c] + [dev_z(dz, dy) for dz, dy in peers]
    for dev in greeted:
        pl.semaphore_signal(barrier, inc=1, device_id=dev, device_id_type=MESH)
    own = uslot(px, pyh, pc)
    load_v = pltpu.make_async_copy(slab_hbm, vbuf.at[own], local_sem.at[2])
    load_v.start()
    load_i = pltpu.make_async_copy(ids_hbm, ids_ref, local_sem.at[3])
    load_i.start()
    load_x = pltpu.make_async_copy(start_hbm, direct.at[0], local_sem.at[1])
    load_x.start()
    load_w = pltpu.make_async_copy(weights_hbm, weights_ref, local_sem.at[0])
    load_w.start()
    load_v.wait()
    pl.semaphore_wait(barrier, len(greeted))

    parts = rows // tile
    sends = []

    def send(src, slot, j, dev, kind):
        copy = pltpu.make_async_remote_copy(
            src_ref=src.at[pl.ds(j * tile, tile)],
            dst_ref=vbuf.at[slot, pl.ds(j * tile, tile)],
            send_sem=g_send.at[kind * parts + j],
            recv_sem=g_recv.at[kind * parts + j],
            device_id=dev,
            device_id_type=MESH,
        )
        copy.start()
        sends.append(copy)

    def arrived(slot, j, kind):
        view = vbuf.at[slot, pl.ds(j * tile, tile)]
        pltpu.make_async_copy(view, view, g_recv.at[kind * parts + j]).wait()

    gram_acc[...] = jnp.zeros_like(gram_acc)

    def convert(src, slot, j):
        high, low = split(src[pl.ds(j * tile, tile), :])
        cat = jnp.concatenate([high, low], axis=1)
        vcat[slot * parts + j] = cat
        gram_acc[...] += lax.dot_general(
            cat, cat, (((0,), (0,)), ((), ())), preferred_element_type=F32
        )

    Y, L0, R0, O0, L1, R1, O1, C0 = range(8)
    for j in range(parts):
        send(vbuf.at[own], own, j, dev_y, Y)
        send(vbuf.at[own], own, j, dev_r, L0)
        send(vbuf.at[own], own, j, dev_l, R0)
        send(vbuf.at[own], own, j, dev_o, O0)
        send(vbuf.at[own], own, j, dev_c, C0)
    for j in range(parts):
        convert(vbuf.at[own], own, j)
    across = uslot(px, qyh, pc)
    for j in range(parts):
        arrived(across, j, Y)
        send(vbuf.at[across], across, j, dev_r, L1)
        send(vbuf.at[across], across, j, dev_l, R1)
        send(vbuf.at[across], across, j, dev_o, O1)
        send(vbuf.at[across], across, j, dev_c, C0 + Y + 1)
    routes = [(xl, pyh, L0), (xr, pyh, R0), (xo, pyh, O0), (xl, qyh, L1), (xr, qyh, R1), (xo, qyh, O1)]
    for x, yh, kind in routes[:3]:
        for j in range(parts):
            slot = uslot(x, yh, pc)
            arrived(slot, j, kind)
            send(vbuf.at[slot], slot, j, dev_c, C0 + kind + 1)
    for x, yh, kind in [(px, qyh, Y)] + routes[:3]:
        for j in range(parts):
            convert(vbuf.at[uslot(x, yh, pc)], uslot(x, yh, pc), j)
    for x, yh, kind in [(px, pyh, -1), (px, qyh, Y)] + routes[:3]:
        for j in range(parts):
            slot = uslot(x, yh, qc)
            arrived(slot, j, C0 + kind + 1)
            convert(vbuf.at[slot], slot, j)
    for j in range(parts):
        for x, yh, kind in routes[3:]:
            slot = uslot(x, yh, pc)
            arrived(slot, j, kind)
            send(vbuf.at[slot], slot, j, dev_c, C0 + kind + 1)
            convert(vbuf.at[slot], slot, j)
    for j in range(parts):
        for x, yh, kind in routes[3:]:
            slot = uslot(x, yh, qc)
            arrived(slot, j, C0 + kind + 1)
            convert(vbuf.at[slot], slot, j)
    for copy in sends:
        copy.wait_send()

    gram = gram_acc[...]
    gram = gram[:tile] + gram[tile:]
    gram = gram[:, :tile] + gram[:, tile:]
    gram_cat[...] = jnp.concatenate(split(gram), axis=1)

    load_i.wait()
    load_x.wait()
    load_w.wait()

    def operand(vec):
        high, low = split(vec)
        lhs = jnp.concatenate(
            [jnp.concatenate([high, high], axis=1), jnp.concatenate([low, low], axis=1)], axis=0
        )
        own_part = jnp.dot(
            jnp.concatenate([high, low], axis=0), gram_cat[...], preferred_element_type=F32
        )
        return lhs, own_part

    def fold(acc):
        acc = acc[:tile] + acc[tile:]
        return acc[:, :tile] + acc[:, tile:]

    def scored(lhs, c, k):
        pair = jnp.concatenate([vcat[ids_ref[c, 0, k]], vcat[ids_ref[c, 0, k + 1]]], axis=0)
        scores = lax.dot_general(lhs, pair, (((1,), (1,)), ((), ())), preferred_element_type=F32)
        base = c * count + k
        wt = jnp.concatenate([weights_ref[base], weights_ref[base + 1]], axis=1)
        return pair, scores[:tile] + scores[tile:], wt

    def image(c, t, first):
        vec = direct[t, c]
        lhs, acc = operand(-vec if first else vec)
        for k in range(0, count, 2):
            pair, scores, wt = scored(lhs, c, k)
            scaled = scores * wt
            if first:
                scaled = scaled + jnp.where(wt > 0, 1.0 + wt, 0.0)
            acc += jnp.dot(
                jnp.concatenate(split(scaled), axis=0), pair, preferred_element_type=F32
            )
        part[c] = fold(acc)

    diagonal = lax.broadcasted_iota(jnp.int32, (tile, tile), 0) == lax.broadcasted_iota(
        jnp.int32, (tile, tile), 1
    )

    def curvature(c):
        vec = direct[ROUNDS, c]
        lhs, own_part = operand(vec)
        acc = None
        for k in range(0, count, 2):
            _, scores, wt = scored(lhs, c, k)
            term = scores * scores * wt
            acc = term if acc is None else acc + term
        share = acc[:, :tile] + acc[:, tile:] + vec * fold(own_part)
        share = jnp.sum(share, axis=1, keepdims=True)
        dots[c, item] = jnp.sum(jnp.where(diagonal, share, 0.0), axis=0, keepdims=True)

    mine = pl.multiple_of(pyl * half, half)
    other = pl.multiple_of((1 - pyl) * half, half)
    zrow = pl.multiple_of(pz * piece, piece)
    prow = pl.multiple_of(pyl * half + pz * piece, piece)

    def copy_y(c):
        return pltpu.make_async_remote_copy(
            src_ref=part.at[c, pl.ds(other, half)],
            dst_ref=ybuf.at[c],
            send_sem=y_send.at[c],
            recv_sem=y_recv.at[c],
            device_id=dev_p,
            device_id_type=MESH,
        )

    def copy_b(c, t):
        return pltpu.make_async_remote_copy(
            src_ref=direct.at[t, c, pl.ds(mine, half)],
            dst_ref=direct.at[t, c, pl.ds(mine, half)],
            send_sem=b_send.at[c],
            recv_sem=b_recv.at[c],
            device_id=dev_p,
            device_id_type=MESH,
        )

    def copy_e(c):
        view = scal.at[c, pl.ds(pyl * NZ, NZ)]
        return pltpu.make_async_remote_copy(
            src_ref=view,
            dst_ref=view,
            send_sem=e_send.at[c],
            recv_sem=e_recv.at[c],
            device_id=dev_p,
            device_id_type=MESH,
        )

    def wait_bytes(view, sem):
        pltpu.make_async_copy(view, view, sem).wait()

    def stage_image(c, t):
        @pl.when(t > 0)
        def _():
            copy_b(c, t).wait()

        @pl.when(t == 0)
        def _():
            image(c, t, True)

        @pl.when(jnp.logical_and(t > 0, t < ROUNDS))
        def _():
            image(c, t, False)

        @pl.when(t < ROUNDS)
        def _():
            copy_y(c).start()

        @pl.when(t == ROUNDS)
        def _():
            copy_e(c).wait()
            curvature(c)
            for dz, dy in peers:
                pltpu.make_async_remote_copy(
                    src_ref=dots.at[c, item],
                    dst_ref=dots.at[c, item],
                    send_sem=d_send.at[c],
                    recv_sem=d_recv.at[c],
                    device_id=dev_z(dz, dy),
                    device_id_type=MESH,
                ).start()

    def stage_sum(c):
        copy_y(c).wait()
        zsum[c] = part[c, pl.ds(mine, half), :] + ybuf[c]
        for dz, dy in column:
            row = pl.multiple_of(place(dz, dy)[0] * piece, piece)
            pltpu.make_async_remote_copy(
                src_ref=zsum.at[c, pl.ds(row, piece)],
                dst_ref=zbuf.at[c, slot_of(dz)],
                send_sem=z_send.at[c],
                recv_sem=z_recv.at[c],
                device_id=dev_z(dz, dy),
                device_id_type=MESH,
            ).start()

    def spread(c, t):
        for dz, dy in column:
            pltpu.make_async_remote_copy(
                src_ref=direct.at[t, c, pl.ds(prow, piece)],
                dst_ref=direct.at[t, c, pl.ds(prow, piece)],
                send_sem=a_send.at[c],
                recv_sem=a_recv.at[c],
                device_id=dev_z(dz, dy),
                device_id_type=MESH,
            ).start()

    seat = pyl * NZ + pz
    lane = lax.broadcasted_iota(jnp.int32, (piece, tile), 1)
    sublane = lax.broadcasted_iota(jnp.int32, (piece, tile), 0)

    def stage_solve(c, t):
        wait_bytes(zbuf.at[c], z_send.at[c])
        wait_bytes(zbuf.at[c], z_recv.at[c])
        got = zsum[c, pl.ds(zrow, piece), :]
        for k in range(NZ - 1):
            got = got + zbuf[c, k]

        @pl.when(t == 0)
        def _():
            r = got - 1.0 * direct[0, c, pl.ds(prow, piece), :]
            rs[c] = r
            ps[c] = r
            norms[c] = jnp.broadcast_to(jnp.sum(r * r, axis=1, keepdims=True), r.shape)
            direct[1, c, pl.ds(prow, piece), :] = r

        @pl.when(t > 0)
        def _():
            p = ps[c]
            q = got + 1.0 * p
            now = norms[c]
            alpha = now / (jnp.sum(p * q, axis=1, keepdims=True) + 1e-06)
            r = rs[c] - alpha * q
            after = jnp.broadcast_to(jnp.sum(r * r, axis=1, keepdims=True), r.shape)
            p = r + after / (now + 1e-06) * p
            rs[c] = r
            ps[c] = p
            norms[c] = after
            direct[t + 1, c, pl.ds(prow, piece), :] = p
            alphas[t, c] = alpha

        spread(c, t + 1)

        @pl.when(t == ROUNDS - 1)
        def _():
            row = norms[c]
            for k in range(ITERS - 1):
                row = jnp.where(lane < (ITERS - 1 - k) * piece, alphas[ITERS - 1 - k, c], row)
            keep = jnp.logical_and(lax.rem(lane, piece) == sublane, lane < ITERS * piece)
            scal[c, seat] = jnp.sum(jnp.where(keep, row, 0.0), axis=0, keepdims=True)
            for dz, dy in column:
                pltpu.make_async_remote_copy(
                    src_ref=scal.at[c, seat],
                    dst_ref=scal.at[c, seat],
                    send_sem=s_send.at[c],
                    recv_sem=s_recv.at[c],
                    device_id=dev_z(dz, dy),
                    device_id_type=MESH,
                ).start()

    def stage_spread(c, t):
        wait_bytes(zbuf.at[c], a_send.at[c])
        wait_bytes(zbuf.at[c], a_recv.at[c])
        copy_b(c, t + 1).start()

        @pl.when(t == ROUNDS - 1)
        def _():
            view = scal.at[c, pl.ds(0, NZ - 1)]
            wait_bytes(view, s_send.at[c])
            wait_bytes(view, s_recv.at[c])
            copy_e(c).start()

    wide_lane = lax.broadcasted_iota(jnp.int32, (tile, tile), 1)
    wide_row = lax.broadcasted_iota(jnp.int32, (tile, tile), 0)

    def stage_last(c):
        rows_of = jnp.concatenate(
            [jnp.broadcast_to(scal[c, g], (piece, tile)) for g in range(NZ * NYL)], axis=0
        )

        def column_of(k):
            keep = wide_lane == lax.rem(wide_row, piece) + k * piece
            return jnp.sum(jnp.where(keep, rows_of, 0.0), axis=1, keepdims=True)

        vec = direct[ROUNDS, c]
        x = direct[0, c]
        for k in range(ITERS - 1):
            x = x + column_of(k) * direct[k + 1, c]
        norm = column_of(ITERS - 1)
        own_dot = jnp.sum(vec * vec, axis=1, keepdims=True)
        view = dots.at[c, pl.ds(0, NZ * NYL - 1)]
        wait_bytes(view, d_send.at[c])
        wait_bytes(view, d_recv.at[c])
        total = jnp.sum(dots[c], axis=0)
        total = jnp.sum(jnp.where(diagonal, total, 0.0), axis=1, keepdims=True)
        part[c] = x + norm / (total + own_dot + 1e-06) * vec
        pltpu.make_async_copy(part.at[c], out_hbm.at[c], out_sem.at[c]).start()

    def guarded(step, offset, rounds, body):
        at = step - offset
        t = lax.div(at, PERIOD)
        c = lax.rem(at, PERIOD)

        @pl.when(jnp.logical_and(at >= 0, jnp.logical_and(t < rounds, c < blocks)))
        def _():
            body(c, t)

    def step_body(step, carry):
        guarded(step, 0, ROUNDS + 1, stage_image)
        guarded(step, AT_SUM, ROUNDS, lambda c, t: stage_sum(c))
        guarded(step, AT_SOLVE, ROUNDS, stage_solve)
        guarded(step, AT_SPREAD, ROUNDS, stage_spread)

        @pl.when(step >= ROUNDS * PERIOD + AT_LAST)
        def _():
            stage_last(step - (ROUNDS * PERIOD + AT_LAST))

        return carry

    lax.fori_loop(0, ROUNDS * PERIOD + AT_LAST + blocks, step_body, 0)
    for c in range(blocks):
        pltpu.make_async_copy(part.at[c], out_hbm.at[c], out_sem.at[c]).wait()


def local(item_factors, weights, tile_ids, start_factors):
    blocks, count, tile, _ = weights.shape
    _, rows, rank = item_factors.shape
    gathered = NX * NYH * NCORE
    half = tile // NYL
    piece = half // NZ
    dma = pltpu.SemaphoreType.DMA
    vmem = pltpu.VMEM
    out = pl.pallas_call(
        functools.partial(kernel, blocks, count),
        out_shape=jax.ShapeDtypeStruct((blocks, tile, rank), F32),
        in_specs=[
            pl.BlockSpec(memory_space=pl.ANY),
            pl.BlockSpec(memory_space=pl.ANY),
            pl.BlockSpec(memory_space=pl.ANY),
            pl.BlockSpec(memory_space=pl.ANY),
        ],
        out_specs=pl.BlockSpec(memory_space=pl.ANY),
        scratch_shapes=[
            pltpu.SMEM((blocks, 1, count), jnp.int32),
            vmem((blocks * count, tile, tile), F32),
            vmem((gathered, rows, rank), F32),
            vmem((gathered * rows // tile, tile, 2 * rank), BF16),
            vmem((2 * rank, 2 * rank), F32),
            vmem((rank, 2 * rank), BF16),
            vmem((ROUNDS + 1, blocks, tile, rank), F32),
            vmem((blocks, tile, rank), F32),
            vmem((blocks, half, rank), F32),
            vmem((blocks, half, rank), F32),
            vmem((blocks, NZ - 1, piece, rank), F32),
            vmem((blocks, NZ * NYL, 1, tile), F32),
            vmem((blocks, NZ * NYL, 1, tile), F32),
            vmem((blocks, piece, rank), F32),
            vmem((blocks, piece, rank), F32),
            vmem((blocks, piece, rank), F32),
            vmem((ROUNDS, blocks, piece, rank), F32),
            dma((4,)),
            dma((blocks,)),
            dma((15 * rows // tile,)),
            dma((15 * rows // tile,)),
        ]
        + [dma((blocks,))] * 14,
        compiler_params=pltpu.CompilerParams(collective_id=0, has_side_effects=True),
        name="als_sweep",
    )(
        tile_ids,
        weights.reshape(blocks * count, tile, tile),
        item_factors.reshape(rows, rank),
        start_factors.reshape(blocks, tile, rank),
    )
    return out.reshape(blocks * tile, rank)


def solution(mesh):
    in_specs = (
        P("item", "user", None),
        P("user", "item", None, None),
        P("user", "item", None),
        P("user", None),
    )
    out_specs = P("user", None)
    return jax.shard_map(local, mesh=mesh, in_specs=in_specs, out_specs=out_specs, check_vma=False)
```

time: 105 us -> 93.8 us (0.89)
  Pallas kernels: 103 us -> 91.6 us
    pallas_call x1, Pallas kernels: 103 us -> 91.6 us  [local(): pl.pallas_call(functools.partial(kernel, blocks, count), out_shape=jax.Sh...]
where the time goes in v3:
time: 93.8 us; the launch traced here: 93.5 us
  Pallas kernels  91.6 us (98%)
  local copies, waits for them, and re-layouts  1.87 us (2%)
    pallas_call x1, Pallas kernels, local(): pl.pallas_call(functools.partial(kernel, blocks, count), out_shape=jax.Sh...  91.6 us

profile of v3, /device:TPU:8, one launch (start us, length us, event | category | flops | bytes accessed | tf_op | source)
XLA Modules:
  0.0 93.5 jit_solution(10626200543073742515)
XLA Ops:
  0.0 91.6 %als_sweep.1 = f32[8,128,128]{2,1,0:T(8,128)} custom-call(s32[8,1,16]{2,1,0:T(1,128)} %ids_hbm.1, f32[128,128,128]{2,1,0:T(8,128)} %bitcast.4, f32[256,128]{1,0:T(8,128)} %bitcast.7, f32[8,128,128]{2,1,0:T(8,128)} %bitcast.6), custom_call_target="tpu_custom_call" | custom-call | tf_op jit(solution)/shard_map/als_sweep/pallas_call | solution.py:479
  91.6 1.9 %copy.6 = f32[1024,128]{1,0:T(8,128)} copy(f32[1024,128]{1,0:T(8,128)} %bitcast.5) | data formatting | bytes 1048576

commit v4 on v3

--- a/solution.py
+++ b/solution.py
@@ -108,8 +108,11 @@
     def slot_of(dz):
         return column.index((NZ - dz, 0))
 
+    zdev = {peer: dev_z(*peer) for peer in peers}
+    zrows = {dz: pl.multiple_of(place(dz, 0)[0] * piece, piece) for dz, _ in column}
+
     barrier = pltpu.get_barrier_semaphore()
-    greeted = [dev_y, dev_l, dev_r, dev_o, dev_c] + [dev_z(dz, dy) for dz, dy in peers]
+    greeted = [dev_y, dev_l, dev_r, dev_o, dev_c] + [zdev[peer] for peer in peers]
     for dev in greeted:
         pl.semaphore_signal(barrier, inc=1, device_id=dev, device_id_type=MESH)
     own = uslot(px, pyh, pc)
@@ -154,30 +157,47 @@
         )
 
     Y, L0, R0, O0, L1, R1, O1, C0 = range(8)
-    for j in range(parts):
-        send(vbuf.at[own], own, j, dev_y, Y)
+    send(vbuf.at[own], own, 0, dev_y, Y)
+    for j in (1, 0):
+        send(vbuf.at[own], own, j, dev_o, O0)
         send(vbuf.at[own], own, j, dev_r, L0)
         send(vbuf.at[own], own, j, dev_l, R0)
-        send(vbuf.at[own], own, j, dev_o, O0)
+    send(vbuf.at[own], own, 1, dev_y, Y)
+    for j in range(parts):
         send(vbuf.at[own], own, j, dev_c, C0)
     for j in range(parts):
         convert(vbuf.at[own], own, j)
     across = uslot(px, qyh, pc)
-    for j in range(parts):
-        arrived(across, j, Y)
-        send(vbuf.at[across], across, j, dev_r, L1)
-        send(vbuf.at[across], across, j, dev_l, R1)
-        send(vbuf.at[across], across, j, dev_o, O1)
-        send(vbuf.at[across], across, j, dev_c, C0 + Y + 1)
     routes = [(xl, pyh, L0), (xr, pyh, R0), (xo, pyh, O0), (xl, qyh, L1), (xr, qyh, R1), (xo, qyh, O1)]
-    for x, yh, kind in routes[:3]:
-        for j in range(parts):
-            slot = uslot(x, yh, pc)
-            arrived(slot, j, kind)
-            send(vbuf.at[slot], slot, j, dev_c, C0 + kind + 1)
-    for x, yh, kind in [(px, qyh, Y)] + routes[:3]:
+
+    def along(x, yh, kind):
+        slot = uslot(x, yh, pc)
+        arrived(slot, 1, kind)
+        send(vbuf.at[slot], slot, 1, dev_y, kind + L1 - L0)
+        send(vbuf.at[slot], slot, 1, dev_c, C0 + kind + 1)
+
+    def pass_on(x, yh, kind, j):
+        slot = uslot(x, yh, pc)
+        arrived(slot, j, kind)
+        send(vbuf.at[slot], slot, j, dev_c, C0 + kind + 1)
+
+    along(*routes[0])
+    along(*routes[1])
+    arrived(across, 0, Y)
+    send(vbuf.at[across], across, 0, dev_o, O1)
+    send(vbuf.at[across], across, 0, dev_r, L1)
+    send(vbuf.at[across], across, 0, dev_l, R1)
+    send(vbuf.at[across], across, 0, dev_c, C0 + Y + 1)
+    along(*routes[2])
+    pass_on(px, qyh, Y, 1)
+    for x, yh, kind in routes[:2]:
+        pass_on(x, yh, kind, 0)
+    for x, yh, kind in [(px, qyh, Y)] + routes[:2]:
         for j in range(parts):
             convert(vbuf.at[uslot(x, yh, pc)], uslot(x, yh, pc), j)
+    pass_on(*routes[2], 0)
+    for j in range(parts):
+        convert(vbuf.at[uslot(xo, pyh, pc)], uslot(xo, pyh, pc), j)
     for x, yh, kind in [(px, pyh, -1), (px, qyh, Y)] + routes[:3]:
         for j in range(parts):
             slot = uslot(x, yh, qc)
@@ -185,10 +205,10 @@
             convert(vbuf.at[slot], slot, j)
     for j in range(parts):
         for x, yh, kind in routes[3:]:
-            slot = uslot(x, yh, pc)
-            arrived(slot, j, kind)
-            send(vbuf.at[slot], slot, j, dev_c, C0 + kind + 1)
-            convert(vbuf.at[slot], slot, j)
+            pass_on(x, yh, kind, j)
+    for x, yh, kind in routes[3:]:
+        for j in range(parts):
+            convert(vbuf.at[uslot(x, yh, pc)], uslot(x, yh, pc), j)
     for j in range(parts):
         for x, yh, kind in routes[3:]:
             slot = uslot(x, yh, qc)
@@ -234,7 +254,7 @@
             pair, scores, wt = scored(lhs, c, k)
             scaled = scores * wt
             if first:
-                scaled = scaled + jnp.where(wt > 0, 1.0 + wt, 0.0)
+                scaled = jnp.where(wt > 0, scaled + (1.0 + wt), 0.0)
             acc += jnp.dot(
                 jnp.concatenate(split(scaled), axis=0), pair, preferred_element_type=F32
             )
@@ -322,7 +342,7 @@
                     dst_ref=dots.at[c, item],
                     send_sem=d_send.at[c],
                     recv_sem=d_recv.at[c],
-                    device_id=dev_z(dz, dy),
+                    device_id=zdev[dz, dy],
                     device_id_type=MESH,
                 ).start()
 
@@ -330,13 +350,12 @@
         copy_y(c).wait()
         zsum[c] = part[c, pl.ds(mine, half), :] + ybuf[c]
         for dz, dy in column:
-            row = pl.multiple_of(place(dz, dy)[0] * piece, piece)
             pltpu.make_async_remote_copy(
-                src_ref=zsum.at[c, pl.ds(row, piece)],
+                src_ref=zsum.at[c, pl.ds(zrows[dz], piece)],
                 dst_ref=zbuf.at[c, slot_of(dz)],
                 send_sem=z_send.at[c],
                 recv_sem=z_recv.at[c],
-                device_id=dev_z(dz, dy),
+                device_id=zdev[dz, dy],
                 device_id_type=MESH,
             ).start()
 
@@ -347,7 +366,7 @@
                 dst_ref=direct.at[t, c, pl.ds(prow, piece)],
                 send_sem=a_send.at[c],
                 recv_sem=a_recv.at[c],
-                device_id=dev_z(dz, dy),
+                device_id=zdev[dz, dy],
                 device_id_type=MESH,
             ).start()
 
@@ -400,7 +419,7 @@
                     dst_ref=scal.at[c, seat],
                     send_sem=s_send.at[c],
                     recv_sem=s_recv.at[c],
-                    device_id=dev_z(dz, dy),
+                    device_id=zdev[dz, dy],
                     device_id_type=MESH,
                 ).start()
 

time: 93.8 us -> 92.7 us (0.988)
  no operation moved by 1% of the time
where the time goes in v4:
time: 92.7 us; the launch traced here: 92.6 us
  Pallas kernels  90.7 us (98%)
  local copies, waits for them, and re-layouts  1.87 us (2%)
    pallas_call x1, Pallas kernels, local(): pl.pallas_call(functools.partial(kernel, blocks, count), out_shape=jax.Sh...  90.7 us
    unnamed x1, local copies, waits for them, and re-layouts  1.87 us

profile of v4, /device:TPU:8, one launch (start us, length us, event | category | flops | bytes accessed | tf_op | source)
XLA Modules:
  0.0 92.6 jit_solution(5120936134911916425)
XLA Ops:
  0.0 90.7 %als_sweep.1 = f32[8,128,128]{2,1,0:T(8,128)} custom-call(s32[8,1,16]{2,1,0:T(1,128)} %ids_hbm.1, f32[128,128,128]{2,1,0:T(8,128)} %bitcast.4, f32[256,128]{1,0:T(8,128)} %bitcast.7, f32[8,128,128]{2,1,0:T(8,128)} %bitcast.6), custom_call_target="tpu_custom_call" | custom-call | tf_op jit(solution)/shard_map/als_sweep/pallas_call | solution.py:498
  90.7 1.9 %copy.6 = f32[1024,128]{1,0:T(8,128)} copy(f32[1024,128]{1,0:T(8,128)} %bitcast.5) | data formatting | bytes 1048576
